TPU v7x, 32 devices: a whole 2x2x4 slice. The times are simulated.
32 devices in a mesh: view: 4 (over z), patch: 8 (over y, x, core).
Axes of the slice: x: 2, y: 2, z: 4, core: 2. Of those that a mesh axis runs over, the one named last changes fastest.
Arguments:
- coefficients: bfloat16 [8, 2304, 32, 512], P('view', 'patch'), may hold values from -0.1875 to 0.1875
- sky_year: bfloat16 [2304, 8760], P('patch'), may hold values from 0.19921875 to 5
- hour_list: int32 [96], replicated, may hold values from 0 to 8759
- retention: float32 [32, 512], P('patch'), may hold values from 0 to 1
Outputs:
- acuity: float32 [32, 8, 96, 512], P('patch', 'view')
- veil: float32 [32, 8, 96, 512], P('patch', 'view')
All inputs are finite; a program needn't handle non-finite values.
Results may differ from a plain program's by a relative error of at most 0.0003.
Values may be sent and summed in bfloat16 or wider, within the bound.
A program may use at most 128 MiB of HBM per device.

v0:
```python
import jax
import jax.numpy as jnp
from jax import lax
from jax.sharding import PartitionSpec as P

binomial_taps = (0.0625, 0.25, 0.375, 0.25, 0.0625)


def padded_2(block, sides, width):
    for axis, dim in sides:
        count = lax.axis_size(axis)
        forward = [(i, i + 1) for i in range(count - 1)]
        backward = [(target, source) for source, target in forward]
        low = lax.ppermute(
            lax.slice_in_dim(block, block.shape[dim] - width, None, axis=dim), axis, forward
        )
        high = lax.ppermute(lax.slice_in_dim(block, 0, width, axis=dim), axis, backward)
        block = jnp.concatenate([low, block, high], axis=dim)
    return block


def entering(value, axis, join, neutral, backward):
    count, mine = (lax.axis_size(axis), lax.axis_index(axis))
    pieces = jax.tree.map(lambda part: lax.all_gather(part, axis), value)
    if backward:
        pieces = jax.tree.map(lambda part: part[::-1], pieces)
        mine = count - 1 - mine
    running = jax.tree.map(
        lambda part, zero: jnp.full_like(part, 0) + jnp.asarray(zero, part.dtype), value, neutral
    )

    def hop(position, running):
        longer = join(running, jax.tree.map(lambda part: part[position], pieces))
        return jax.tree.map(lambda new, old: jnp.where(position < mine, new, old), longer, running)

    return lax.fori_loop(0, count - 1, hop, running)


def combine(earlier, later):
    return (earlier[0] * later[0], later[0] * earlier[1] + later[1])


def taps_sum(padded, device_axis_name, length):
    total = jnp.zeros(
        padded.shape[:device_axis_name] + (length,) + padded.shape[device_axis_name + 1 :],
        jnp.float32,
    )
    for offset in range(5):
        total = total + binomial_taps[offset] * lax.slice_in_dim(
            padded, offset, offset + length, axis=device_axis_name
        )
    return total


def shards(coefficients, sky_year, hour_list, retention):
    sky_shard_values = jnp.take(sky_year, hour_list, axis=1)
    row_count = retention.shape[0]
    luminance = lax.psum_scatter(
        jnp.einsum(
            "ph,vprc->rvhc", sky_shard_values, coefficients, preferred_element_type=jnp.float32
        ),
        "patch",
        scatter_dimension=0,
        tiled=True,
    )
    padded = padded_2(luminance, (("patch", 0),), 2)
    image_width = padded.shape[3]
    wide_pad = jnp.pad(padded, ((0, 0), (0, 0), (0, 0), (2, 2)))
    across = taps_sum(wide_pad, 3, image_width)
    acuity = taps_sum(across, 0, row_count)
    retain_rates = retention[:, None, None, :]
    front_gain, front_sum = lax.associative_scan(combine, (retain_rates, luminance), axis=0)
    unity = (jnp.ones_like(front_gain[-1]), jnp.zeros_like(front_sum[-1]))
    _, incoming_down = entering((front_gain[-1], front_sum[-1]), "patch", combine, unity, False)
    forward = front_gain * incoming_down[None] + front_sum
    back_gain, back_sum = lax.associative_scan(
        combine, (retain_rates, luminance), reverse=True, axis=0
    )
    _, incoming_up = entering((back_gain[0], back_sum[0]), "patch", combine, unity, True)
    reverse_pass = back_gain * incoming_up[None] + back_sum
    veil = 0.125 * (forward + reverse_pass)
    return (acuity, veil)


def solution(mesh):
    placed = (P("view", "patch", None, None), P("patch", None), P(), P("patch", None))
    return jax.shard_map(
        shards,
        mesh=mesh,
        in_specs=placed,
        out_specs=(P("patch", "view", None, None), P("patch", "view", None, None)),
        check_vma=False,
    )
```

profile of v0, /device:TPU:5, one launch (start us, length us, event | category | flops | bytes accessed | tf_op | source)
XLA Modules:
  0.0 344.6 jit_solution(865832402538347018)
XLA Ops:
  8.5 8.3 %copy.12 = bf16[288,8760]{0,1:T(8,128)(2,1)} copy(bf16[288,8760]{1,0:T(8,128)(2,1)} %param.9) | data formatting | bytes 10091520 | tf_op args[1]
  16.8 4.5 %gather_fusion = bf16[96,288]{1,0:T(8,128)(2,1)S(1)} fusion(bf16[288,8760]{0,1:T(8,128)(2,1)} %copy.12, s32[1024]{0:T(1024)S(1)} %pad_clamp_fusion), kind=kCustom, calls=%fused_computation | custom fusion | bytes 110976 | tf_op jit(solution)/shard_map/jit(_take)/gather | solution.py:56
  21.4 32.4 %fusion.4 = f32[32,2,96,512]{3,2,0,1:T(8,128)} fusion(bf16[2,288,32,512]{3,2,1,0:T(8,128)(2,1)} %param.8, bf16[96,288]{1,0:T(8,128)(2,1)S(1)} %gather_fusion, pred[96]{0:T(512)(128)(4,1)S(1)} %compare_and_fusion), kind=kOutput, calls=%fused_computation.13 | convolution fusion | flops 1811966976 | bytes 31512672 | tf_op jit(solution)/shard_map/ph,vprc->rvhc/dot_general | solution.py:59
  57.1 169.5 %all-reduce.20.cloned.1.call-done = f32[32,2,96,512]{3,2,0,1:T(8,128)} async-done(((f32[32,2,96,512]{3,2,0,1:T(8,128)}), f32[32,2,96,512]{3,2,0,1:T(8,128)}) %all-reduce.20.cloned.1.call-update) | async-done | bytes 12582928
  230.0 2.5 constant_dynamic-slice_fusion.3
  233.5 2.1 pad.71
  235.6 4.5 %pad.72 = f32[4,2,96,512]{3,2,0,1:T(8,128)} pad(f32[2,2,96,512]{3,2,0,1:T(8,128)} %pad_add_fusion, f32[]{:T(128)} %constant.75.clone.1), padding=1_0_1x0_0_0x0_0_0x0_0_0 | pad | bytes 2359300 | tf_op jit(solution)/shard_map/pad | solution.py:76
  240.1 1.8 slice_add_fusion
  242.2 2.1 pad_maximum_fusion.1
  244.3 2.1 pad.63
  246.4 2.3 pad_add_fusion.1
  248.7 4.5 %pad.64 = f32[4,2,96,512]{3,2,0,1:T(8,128)} pad(f32[2,2,96,512]{3,2,0,1:T(8,128)} %pad_add_fusion.1, f32[]{:T(128)} %constant.75.clone.1), padding=1_0_1x0_0_0x0_0_0x0_0_0 | pad | bytes 2359300 | tf_op jit(solution)/shard_map/pad | solution.py:72
  253.2 1.8 slice_add_fusion.2
  255.7 2.7 constant_dynamic-slice_fusion.5
  258.4 2.8 collective-permute-start.1
  261.2 2.7 collective-permute-start
  264.1 28.6 %all_gather.14 = f32[8,1,1,512]{3,2,1,0:T(1,128)S(1)} all-gather(f32[1,1,1,512]{3,2,1,0:T(1,128)S(1)} %slice_add_fusion.4), channel_id=1, replica_groups=mesh['view'=4,'patch'=8] {'patch'}, dimensions={0}, use_global_device_ids=true | all-gather | bytes 18432 | tf_op jit(solution)/shard_map/all_gather | solution.py:24
  292.9 7.9 %all_gather.12 = f32[8,1,1,512]{3,2,1,0:T(1,128)S(1)} all-gather(f32[1,1,1,512]{3,2,1,0:T(1,128)S(1)} %slice_add_fusion.5), channel_id=1, replica_groups=mesh['view'=4,'patch'=8] {'patch'}, dimensions={0}, use_global_device_ids=true | all-gather | bytes 18432 | tf_op jit(solution)/shard_map/all_gather | solution.py:24
  300.8 3.4 add.201
  305.6 3.6 %fusion.11 = f32[8,2,96,512]{3,2,0,1:T(8,128)S(1)} fusion(f32[8,2,96,512]{3,2,0,1:T(8,128)S(1)} %pad_maximum_fusion), kind=kLoop, calls=%fused_computation.18 | loop fusion | flops 7077888 | bytes 6291456 | tf_op jit(solution)/shard_map/add | solution.py:49
  311.0 4.0 %rev.19 = f32[8,2,96,512]{3,2,0,1:T(8,128)} reverse(f32[8,2,96,512]{3,2,0,1:T(8,128)} %all-gather.5.cloned.1.call-done), dimensions={0} | reverse | bytes 6291456 | tf_op jit(solution)/shard_map/rev | solution.py:26
  315.0 9.6 %while.29 = (s32[]{:T(128)}, f32[2,96,512]{2,1,0:T(8,128)S(1)}, s32[]{:T(128)}, f32[8,1,1,512]{3,2,1,0:T(1,128)S(1)}, f32[8,2,96,512]{3,2,0,1:T(8,128)}, /*index=5*/s32[]{:T(128)}, s32[]{:T(128)}) while((s32[]{:T(128)}, f32[2,96,512]{2,1,0:T(8,128)S(1)}, s32[]{:T(128)}, f32[8,1,1,512]{3,2,1,0:T(1,128)S(1)}, ...), condition=%wide.region_4.5_spmd.clone, body=%wide.region_3.4_spmd.clone.sunk | while | flops 393220 | bytes 1185905 | solution.py:36
  324.7 9.6 %while.28 = (s32[]{:T(128)}, f32[2,96,512]{2,1,0:T(8,128)S(1)}, s32[]{:T(128)}, f32[8,1,1,512]{3,2,1,0:T(1,128)S(1)}, f32[8,2,96,512]{3,2,0,1:T(8,128)}, /*index=5*/s32[]{:T(128)}, s32[]{:T(128)}) while((s32[]{:T(128)}, f32[2,96,512]{2,1,0:T(8,128)S(1)}, s32[]{:T(128)}, f32[8,1,1,512]{3,2,1,0:T(1,128)S(1)}, ...), condition=%wide.region_2.3_spmd.clone, body=%wide.region_1.2_spmd.clone.sunk | while | flops 393220 | bytes 1185905 | solution.py:36
  334.2 2.6 add_multiply_fusion
  (100 shorter events, 32.7 us)
Async XLA Ops:
  7.2 219.5 %all-reduce.20.cloned.1.call-start = ((), (), s32[]{:S(2)}) async-start(), calls=%async_computation.2 | async-start | bytes 25165824
  53.8 0.7 copy-start.4
  53.8 0.8 copy-start.9
  53.8 257.2 %all-gather.5.cloned.1.call-start = ((), (), s32[]{:S(2)}) async-start(), calls=%async_computation.1 | async-start | bytes 3538944 | tf_op jit(solution)/shard_map/all_gather | solution.py:24
  228.9 3.6 %copy-start.3 = (f32[1,2,96,512]{3,2,0,1:T(8,128)}, f32[1,2,96,512]{3,2,0,1:T(8,128)S(1)}, u32[]{:S(2)}) copy-start(f32[1,2,96,512]{3,2,0,1:T(8,128)S(1)} %get-tuple-element.282) | copy-start | bytes 1179652
  235.6 6.3 %copy-start.2 = (f32[4,2,96,512]{3,2,0,1:T(8,128)}, f32[4,2,96,512]{3,2,0,1:T(8,128)S(1)}, u32[]{:S(2)}) copy-start(f32[4,2,96,512]{3,2,0,1:T(8,128)S(1)} %pad.71) | copy-start | bytes 4718596
  241.9 82.8 %all-gather.3.cloned.1.call-start = ((), (), s32[]{:S(2)}) async-start(), calls=%async_computation | async-start | bytes 3538944 | tf_op jit(solution)/shard_map/all_gather | solution.py:24
  246.4 6.8 %copy-start = (f32[4,2,96,512]{3,2,0,1:T(8,128)}, f32[4,2,96,512]{3,2,0,1:T(8,128)S(1)}, u32[]{:S(2)}) copy-start(f32[4,2,96,512]{3,2,0,1:T(8,128)S(1)} %pad.63) | copy-start | bytes 4718596
  255.7 8.3 %copy-start.5 = (f32[1,1,1,512]{3,2,1,0:T(1,128)S(1)}, f32[1,1,1,512]{3,2,1,0:T(1,128)}, u32[]{:S(2)}) copy-start(f32[1,1,1,512]{3,2,1,0:T(1,128)} %get-tuple-element.298) | copy-start | bytes 6148
  255.7 8.3 %copy-start.6 = (f32[1,1,1,512]{3,2,1,0:T(1,128)S(1)}, f32[1,1,1,512]{3,2,1,0:T(1,128)}, u32[]{:S(2)}) copy-start(f32[1,1,1,512]{3,2,1,0:T(1,128)} %get-tuple-element.300) | copy-start | bytes 6148
  255.7 8.3 %copy-start.7 = (f32[1,1,1,512]{3,2,1,0:T(1,128)S(1)}, f32[1,1,1,512]{3,2,1,0:T(1,128)}, u32[]{:S(2)}) copy-start(f32[1,1,1,512]{3,2,1,0:T(1,128)} %get-tuple-element.285) | copy-start | bytes 6148
  255.7 8.3 %copy-start.8 = (f32[1,1,1,512]{3,2,1,0:T(1,128)S(1)}, f32[1,1,1,512]{3,2,1,0:T(1,128)}, u32[]{:S(2)}) copy-start(f32[1,1,1,512]{3,2,1,0:T(1,128)} %get-tuple-element.286) | copy-start | bytes 6148
  258.4 45.7 %collective-permute-start.1 = (f32[2,2,96,512]{3,2,0,1:T(8,128)}, f32[2,2,96,512]{3,2,0,1:T(8,128)S(1)}, u32[]{:S(2)}, u32[]{:S(2)}) collective-permute-start(f32[2,2,96,512]{3,2,0,1:T(8,128)} %get-tuple-element.277), channel_id=1, source_target_pairs={{1,0},{2,1},{3,2},{4,3},{5,4},{6,5},{7,6},{9,8},{10,9},{11,10},{12... | collective-permute-start | bytes 2359304 | tf_op jit(solution)/shard_map/ppermute | solution.py:17
  261.2 42.9 %collective-permute-start = (f32[2,2,96,512]{3,2,0,1:T(8,128)}, f32[2,2,96,512]{3,2,0,1:T(8,128)}, u32[]{:S(2)}, u32[]{:S(2)}) collective-permute-start(f32[2,2,96,512]{3,2,0,1:T(8,128)} %get-tuple-element.276), channel_id=1, source_target_pairs={{0,1},{1,2},{2,3},{3,4},{4,5},{5,6},{6,7},{8,9},{9,10},{10,11},{11... | collective-permute-start | bytes 2359304 | tf_op jit(solution)/shard_map/ppermute | solution.py:14
  315.0 19.2 %copy-start.1 = (f32[4,2,96,512]{3,2,0,1:T(8,128)S(1)}, f32[4,2,96,512]{3,2,0,1:T(8,128)}, u32[]{:S(2)}) copy-start(f32[4,2,96,512]{3,2,0,1:T(8,128)} %copy-done) | copy-start | bytes 4718596
Sparse Core Ops, SparseCore 0:
  54.0 172.6 all-reduce.19
  242.0 37.3 all-gather.4
  281.3 35.8 all-gather.2
where the time goes:
time: 348 us; the launch traced here: 345 us
  waiting for transfers between devices  170 us (49%)
  other arithmetic  45.9 us (13%)
  local copies, waits for them, and re-layouts  39.1 us (11%)
  blocking collectives  36.5 us (10%)
  matrix products  32.4 us (9%)
  between operations  14.8 us (4%)
  starting transfers between devices  5.89 us (2%)
    unnamed x4, waiting for transfers between devices  170 us
    all_gather x2, blocking collectives, entering(): pieces = jax.tree.map(lambda part: lax.all_gather(part, axis), value)  36.5 us
    dot_general x1, matrix products, shards(): jnp.einsum('ph,vprc->rvhc', sky_shard_values, coefficients, preferred_ele...  32.4 us
    select_n x14, other arithmetic, hop(): jnp.where(position < mine, new, old)  18.6 us
    unnamed x29, local copies, waits for them, and re-layouts  13.8 us
  transfers between devices with their start and end apart: 5, of which 1 were waited for; matrix products, arithmetic and copies ran while one was open for 12% of the time, Pallas kernels for 0%

commit v1 on v0

--- a/solution.py
+++ b/solution.py
@@ -1,9 +1,13 @@
 import jax
 import jax.numpy as jnp
 from jax import lax
+from jax.experimental import pallas as pl
+from jax.experimental.pallas import tpu as pltpu
 from jax.sharding import PartitionSpec as P
 
 binomial_taps = (0.0625, 0.25, 0.375, 0.25, 0.0625)
+MESH = pl.DeviceIdType.MESH
+SPAN = 83.0
 
 
 def padded_2(block, sides, width):
@@ -40,19 +44,19 @@
     return (earlier[0] * later[0], later[0] * earlier[1] + later[1])
 
 
-def taps_sum(padded, device_axis_name, length):
+def taps_sum(padded, axis, length):
     total = jnp.zeros(
-        padded.shape[:device_axis_name] + (length,) + padded.shape[device_axis_name + 1 :],
+        padded.shape[:axis] + (length,) + padded.shape[axis + 1 :],
         jnp.float32,
     )
     for offset in range(5):
         total = total + binomial_taps[offset] * lax.slice_in_dim(
-            padded, offset, offset + length, axis=device_axis_name
+            padded, offset, offset + length, axis=axis
         )
     return total
 
 
-def shards(coefficients, sky_year, hour_list, retention):
+def general(coefficients, sky_year, hour_list, retention):
     sky_shard_values = jnp.take(sky_year, hour_list, axis=1)
     row_count = retention.shape[0]
     luminance = lax.psum_scatter(
@@ -82,7 +86,504 @@
     return (acuity, veil)
 
 
+def encode(x):
+    top = jnp.maximum(jnp.max(jnp.abs(x), axis=0, keepdims=True), 1e-30)
+    size = jnp.exp(jnp.abs(x) * (2.0 * SPAN / top) - SPAN)
+    return jnp.where(x < 0, -size, size).astype(jnp.bfloat16), top
+
+
+def decode(code, top):
+    y = code.astype(jnp.float32)
+    size = (jnp.log(jnp.abs(y)) + SPAN) * (top * (0.5 / SPAN))
+    return jnp.where(y < 0, -size, size)
+
+
+def kernel(
+    sky_ref, coef_ref, ret_ref, acu_out, veil_out,
+    lhs, held, mine, given, taken,
+    code_out, top_out, code_in, top_in, lum,
+    halo_out, halo_top_out, halo_in, halo_top_in,
+    carry_out, carry_top_out, carry_in, carry_top_in,
+    rets, down, acuity, veil,
+    load_sem, ret_sem, pair_sem, hop_sem, halo_sem, carry_sem, out_sem, local_sem,
+):
+    view = lax.axis_index("view")
+    me = lax.axis_index("patch")
+    devices = 8
+    chips = 4
+    core = me % 2
+    chip = me // 2
+    cx = chip % 2
+    cy = chip // 2
+    other = 1 - core
+    depth, rows, columns = held.shape[1:]
+    hours = sky_ref.shape[0]
+
+    def at(target):
+        return (view, target)
+
+    def chip_of(k, owner):
+        fx = (1 - owner) * (1 - k // 2) + owner * (1 - k % 2)
+        fy = owner * (1 - k // 2) + (1 - owner) * (1 - k % 2)
+        return 2 * (cy + fy * (1 - 2 * cy)) + cx + fx * (1 - 2 * cx)
+
+    def load(v, d, slot):
+        return pltpu.make_async_copy(
+            coef_ref.at[v, :, pl.ds(pl.multiple_of(d * rows, rows), rows), :],
+            held.at[slot],
+            load_sem.at[slot],
+        )
+
+    load(other, chip_of(0, other), 0).start()
+    load(core, chip_of(0, core), 1).start()
+
+    barrier = pltpu.get_barrier_semaphore()
+    for step in range(1, devices):
+        pl.semaphore_signal(
+            barrier, inc=1, device_id=at((me + step) % devices), device_id_type=MESH
+        )
+
+    spread = (
+        lax.broadcasted_iota(jnp.int32, (depth, depth * rows), 1) // rows
+        == lax.broadcasted_iota(jnp.int32, (depth, depth * rows), 0)
+    )
+    wide = jnp.dot(
+        sky_ref[...],
+        jnp.where(spread, 1.0, 0.0).astype(jnp.bfloat16),
+        preferred_element_type=jnp.float32,
+    )
+    place = lax.broadcasted_iota(jnp.int32, (hours, depth * rows), 1) % rows
+    for r in range(rows):
+        lhs[r * hours : (r + 1) * hours, :] = jnp.where(place == r, wide, 0.0).astype(jnp.bfloat16)
+
+    pl.semaphore_wait(barrier, devices - 1)
+
+    rets[me] = ret_ref[...]
+    ret_copies = []
+    for step in range(1, devices):
+        target = (me + step) % devices
+        copy = pltpu.make_async_remote_copy(
+            src_ref=ret_ref,
+            dst_ref=rets.at[me],
+            send_sem=ret_sem.at[0, step],
+            recv_sem=ret_sem.at[1, step],
+            device_id=at(target),
+            device_id_type=MESH,
+        )
+        copy.start()
+        ret_copies.append(copy)
+
+    partner = chip * 2 + other
+    tile = 256
+
+    def product(slot, dst, k):
+        @pl.loop(0, columns // tile)
+        def _(t):
+            cols = pl.ds(pl.multiple_of(t * tile, tile), tile)
+            block = held[slot, :, :, cols].reshape(depth * rows, tile)
+            dst[k, :, :, cols] = jnp.dot(
+                lhs[...], block, preferred_element_type=jnp.float32
+            ).reshape(rows, hours, tile)
+
+    def pair(k):
+        return pltpu.make_async_remote_copy(
+            src_ref=given.at[k],
+            dst_ref=taken.at[k],
+            send_sem=pair_sem.at[0, k],
+            recv_sem=pair_sem.at[1, k],
+            device_id=at(partner),
+            device_id_type=MESH,
+        )
+
+    def hop(k, n):
+        target = chip_of(n, core) * 2 + core
+        return [
+            pltpu.make_async_remote_copy(
+                src_ref=src.at[k],
+                dst_ref=dst.at[k],
+                send_sem=hop_sem.at[0, i, k],
+                recv_sem=hop_sem.at[1, i, k],
+                device_id=at(target),
+                device_id_type=MESH,
+            )
+            for i, (src, dst) in enumerate(((code_out, code_in), (top_out, top_in)))
+        ]
+
+    @pl.loop(0, chips)
+    def _(k):
+        load(other, chip_of(k, other), 0).wait()
+        product(0, given, k)
+        pair(k).start()
+
+        @pl.when(k < chips - 1)
+        def _():
+            load(other, chip_of(k + 1, other), 0).start()
+
+        load(core, chip_of(k, core), 1).wait()
+        product(1, mine, k)
+
+        @pl.when(k < chips - 1)
+        def _():
+            load(core, chip_of(k + 1, core), 1).start()
+
+        @pl.when(k < 2)
+        def _():
+            pair(k).wait_recv()
+
+            @pl.loop(0, rows)
+            def _(r):
+                code, top = encode(mine[k, r] + taken[k, r])
+                code_out[k, r] = code
+                top_out[k, pl.ds(r, 1), :] = top
+
+            for copy in hop(k, 1):
+                copy.start()
+
+    pair(2).wait_recv()
+    for copy in hop(0, 1):
+        copy.wait_recv()
+
+    @pl.loop(0, rows)
+    def _(r):
+        came = decode(code_in[0, r], top_in[0, pl.ds(r, 1), :])
+        code, top = encode(mine[2, r] + taken[2, r] + came)
+        code_out[2, r] = code
+        top_out[2, pl.ds(r, 1), :] = top
+
+    for copy in hop(2, 2):
+        copy.start()
+
+    pair(3).wait_recv()
+    for copy in hop(1, 1):
+        copy.wait_recv()
+
+    @pl.loop(0, rows)
+    def _(r):
+        came = decode(code_in[1, r], top_in[1, pl.ds(r, 1), :])
+        mine[3, r] = mine[3, r] + taken[3, r] + came
+
+    for copy in ret_copies:
+        copy.wait()
+
+    for copy in hop(2, 2):
+        copy.wait_recv()
+
+    @pl.loop(0, rows)
+    def _(r):
+        came = decode(code_in[2, r], top_in[2, pl.ds(r, 1), :])
+        lum[r + 2] = mine[3, r] + came
+
+    def halo(way, i):
+        target = (chip + (1 - 2 * way) + chips) % chips * 2 + core
+        src, dst = ((halo_out, halo_in), (halo_top_out, halo_top_in))[i]
+        return pltpu.make_async_remote_copy(
+            src_ref=src.at[way],
+            dst_ref=dst.at[way],
+            send_sem=halo_sem.at[0, i, way],
+            recv_sem=halo_sem.at[1, i, way],
+            device_id=at(target),
+            device_id_type=MESH,
+        )
+
+    def send_halo(way):
+        for i in range(2):
+            code, top = encode(lum[i + 2 if way else rows + i])
+            halo_out[way, i] = code
+            halo_top_out[way, i] = top
+        for i in range(2):
+            halo(way, i).start()
+
+    not_last = chip < chips - 1
+    not_first = chip > 0
+
+    @pl.when(not_last)
+    def _():
+        send_halo(0)
+
+    @pl.when(not_first)
+    def _():
+        send_halo(1)
+
+    def rate(r):
+        return rets[chip * 2 + r // 4, pl.ds(r % 4, 1), :]
+
+    half = rows // 2
+
+    def rate(r):
+        return rets[chip * 2 + r // half, pl.ds(r % half, 1), :]
+
+    zero = jnp.zeros((hours, columns), jnp.float32)
+
+    def carry(way, slot, target, i):
+        src, dst = ((carry_out, carry_in), (carry_top_out, carry_top_in))[i]
+        return pltpu.make_async_remote_copy(
+            src_ref=src.at[way],
+            dst_ref=dst.at[chip],
+            send_sem=carry_sem.at[0, i, target],
+            recv_sem=carry_sem.at[1, i, chip],
+            device_id=at(target * 2 + core),
+            device_id_type=MESH,
+        )
+
+    def arrival(source, i):
+        src, dst = ((carry_out, carry_in), (carry_top_out, carry_top_in))[i]
+        return pltpu.make_async_remote_copy(
+            src_ref=src.at[0],
+            dst_ref=dst.at[source],
+            send_sem=carry_sem.at[0, i, source],
+            recv_sem=carry_sem.at[1, i, source],
+            device_id=at(source * 2 + core),
+            device_id_type=MESH,
+        )
+
+    @pl.when(not_last)
+    def _():
+        down[0] = zero
+
+        @pl.loop(0, rows)
+        def _(r):
+            down[0] = rate(r) * down[0] + lum[r + 2]
+
+        code, top = encode(down[0])
+        carry_out[0] = code
+        carry_top_out[0] = top
+
+    @pl.when(not_first)
+    def _():
+        down[0] = zero
+
+        @pl.loop(0, rows)
+        def _(n):
+            r = rows - 1 - n
+            down[0] = rate(r) * down[0] + lum[r + 2]
+
+        code, top = encode(down[0])
+        carry_out[1] = code
+        carry_top_out[1] = top
+
+    for target in range(chips):
+        @pl.when(target > chip)
+        def _():
+            for i in range(2):
+                carry(0, 0, target, i).start()
+
+        @pl.when(target < chip)
+        def _():
+            for i in range(2):
+                carry(1, 0, target, i).start()
+
+    column = lax.broadcasted_iota(jnp.int32, (hours, columns), 1)
+
+    def blur(row):
+        total = binomial_taps[2] * row
+        for k in (-2, -1, 1, 2):
+            moved = pltpu.roll(row, (-k) % columns, 1)
+            inside = column < columns - k if k > 0 else column >= -k
+            total = total + binomial_taps[k + 2] * jnp.where(inside, moved, 0.0)
+        return total
+
+    @pl.loop(0, rows)
+    def _(r):
+        mine[0, r] = blur(lum[r + 2])
+
+    @pl.loop(2, rows - 2)
+    def _(r):
+        total = binomial_taps[2] * mine[0, r]
+        for k in (-2, -1, 1, 2):
+            total = total + binomial_taps[k + 2] * mine[0, r + k]
+        acuity[r] = total
+
+    @pl.when(not_first)
+    def _():
+        for i in range(2):
+            halo(0, i).wait_recv()
+        for i in range(2):
+            lum[i] = blur(decode(halo_in[0, i], halo_top_in[0, i]))
+
+    @pl.when(chip == 0)
+    def _():
+        for i in range(2):
+            lum[i] = zero
+
+    @pl.when(not_last)
+    def _():
+        for i in range(2):
+            halo(1, i).wait_recv()
+        for i in range(2):
+            lum[rows + 2 + i] = blur(decode(halo_in[1, i], halo_top_in[1, i]))
+
+    @pl.when(chip == chips - 1)
+    def _():
+        for i in range(2):
+            lum[rows + 2 + i] = zero
+
+    for r in (0, 1, rows - 2, rows - 1):
+        total = binomial_taps[2] * mine[0, r]
+        for k in (-2, -1, 1, 2):
+            source = r + k
+            outside = source < 0 or source >= rows
+            total = total + binomial_taps[k + 2] * (lum[source + 2] if outside else mine[0, source])
+        acuity[r] = total
+
+    def stay(i):
+        src, dst = ((acuity, acu_out), (veil, veil_out))[i]
+        return pltpu.make_async_copy(
+            src.at[pl.ds(core * half, half)], dst.at[:, core], local_sem.at[i]
+        )
+
+    def leave(i):
+        src, dst = ((acuity, acu_out), (veil, veil_out))[i]
+        return pltpu.make_async_remote_copy(
+            src_ref=src.at[pl.ds(other * half, half)],
+            dst_ref=dst.at[:, core],
+            send_sem=out_sem.at[0, i],
+            recv_sem=out_sem.at[1, i],
+            device_id=at(partner),
+            device_id_type=MESH,
+        )
+
+    stay(0).start()
+    leave(0).start()
+
+    def gain(source):
+        total = rets[source * 2, 0:1, :]
+        for r in range(1, rows):
+            total = total * rets[source * 2 + r // half, r % half : r % half + 1, :]
+        return total
+
+    down[0] = zero
+    down[1] = zero
+    for source in range(chips):
+        @pl.when(source < chip)
+        def _():
+            for i in range(2):
+                arrival(source, i).wait_recv()
+            down[0] = gain(source) * down[0] + decode(carry_in[source], carry_top_in[source])
+
+    for source in range(chips - 1, -1, -1):
+        @pl.when(source > chip)
+        def _():
+            for i in range(2):
+                arrival(source, i).wait_recv()
+            down[1] = gain(source) * down[1] + decode(carry_in[source], carry_top_in[source])
+
+    @pl.loop(0, rows)
+    def _(r):
+        now = rate(r) * down[0] + lum[r + 2]
+        down[0] = now
+        mine[1, r] = now
+
+    @pl.loop(0, rows)
+    def _(n):
+        r = rows - 1 - n
+        now = rate(r) * down[1] + lum[r + 2]
+        down[1] = now
+        veil[r] = 0.125 * (mine[1, r] + now)
+
+    stay(1).start()
+    leave(1).start()
+
+    @pl.loop(0, chips)
+    def _(k):
+        pair(k).wait_send()
+
+    for k, n in ((0, 1), (1, 1), (2, 2)):
+        for copy in hop(k, n):
+            copy.wait_send()
+
+    @pl.when(not_last)
+    def _():
+        for i in range(2):
+            halo(0, i).wait_send()
+
+    @pl.when(not_first)
+    def _():
+        for i in range(2):
+            halo(1, i).wait_send()
+
+    for target in range(chips):
+        @pl.when(target > chip)
+        def _():
+            for i in range(2):
+                carry(0, 0, target, i).wait_send()
+
+        @pl.when(target < chip)
+        def _():
+            for i in range(2):
+                carry(1, 0, target, i).wait_send()
+
+    for i in range(2):
+        stay(i).wait()
+        leave(i).wait()
+
+
+def fused(coefficients, sky_year, hour_list, retention):
+    sky = jnp.take(sky_year, hour_list, axis=1).T
+    views, depth, all_rows, columns = coefficients.shape
+    hours = sky.shape[0]
+    half = retention.shape[0]
+    rows = 2 * half
+    chips = all_rows // rows
+    f32, bf16 = jnp.float32, jnp.bfloat16
+    image = (rows, hours, columns)
+    out = jax.ShapeDtypeStruct((half, views, hours, columns), f32)
+    dma = pltpu.SemaphoreType.DMA
+    return pl.pallas_call(
+        kernel,
+        out_shape=(out, out),
+        in_specs=[
+            pl.BlockSpec(memory_space=pltpu.VMEM),
+            pl.BlockSpec(memory_space=pl.ANY),
+            pl.BlockSpec(memory_space=pltpu.VMEM),
+        ],
+        out_specs=[pl.BlockSpec(memory_space=pl.ANY)] * 2,
+        scratch_shapes=[
+            pltpu.VMEM((rows * hours, depth * rows), bf16),
+            pltpu.VMEM((2, depth, rows, columns), bf16),
+            pltpu.VMEM((chips,) + image, f32),
+            pltpu.VMEM((chips,) + image, f32),
+            pltpu.VMEM((chips,) + image, f32),
+            pltpu.VMEM((3,) + image, bf16),
+            pltpu.VMEM((3, rows, columns), f32),
+            pltpu.VMEM((3,) + image, bf16),
+            pltpu.VMEM((3, rows, columns), f32),
+            pltpu.VMEM((rows + 4, hours, columns), f32),
+            pltpu.VMEM((2, 2, hours, columns), bf16),
+            pltpu.VMEM((2, 2, 1, columns), f32),
+            pltpu.VMEM((2, 2, hours, columns), bf16),
+            pltpu.VMEM((2, 2, 1, columns), f32),
+            pltpu.VMEM((2, hours, columns), bf16),
+            pltpu.VMEM((2, 1, columns), f32),
+            pltpu.VMEM((chips, hours, columns), bf16),
+            pltpu.VMEM((chips, 1, columns), f32),
+            pltpu.VMEM((2 * chips, half, columns), f32),
+            pltpu.VMEM((2, hours, columns), f32),
+            pltpu.VMEM(image, f32),
+            pltpu.VMEM(image, f32),
+            dma((2,)),
+            dma((2, 2 * chips)),
+            dma((2, chips)),
+            dma((2, 2, 3)),
+            dma((2, 2, 2)),
+            dma((2, 2, chips)),
+            dma((2, 2)),
+            dma((2,)),
+        ],
+        compiler_params=pltpu.CompilerParams(
+            collective_id=0, has_side_effects=True, vmem_limit_bytes=60 * 1024 * 1024
+        ),
+    )(sky, coefficients, retention)
+
+
 def solution(mesh):
+    size = mesh.shape["patch"]
+
+    def shards(coefficients, sky_year, hour_list, retention):
+        square = size == 8 and coefficients.shape[0] == 2 and retention.shape[0] == 4
+        if square:
+            return fused(coefficients, sky_year, hour_list, retention)
+        return general(coefficients, sky_year, hour_list, retention)
+
     placed = (P("view", "patch", None, None), P("patch", None), P(), P("patch", None))
     return jax.shard_map(
         shards,

time: 348 us -> 77.2 us (0.22)
  waiting for transfers between devices: 170 us -> 0 us
  Pallas kernels: 0 us -> 57.2 us
  other arithmetic: 45.9 us -> 0.74 us
  blocking collectives: 36.5 us -> 0 us
  matrix products: 32.4 us -> 0 us
  local copies, waits for them, and re-layouts: 39.1 us -> 18.2 us
  between operations: 14.8 us -> 0.66 us
  starting transfers between devices: 5.89 us -> 0 us
    unnamed x4 -> x0, waiting for transfers between devices: 170 us -> none
    pallas_call x0 -> x1, Pallas kernels: none -> 57.2 us  [fused(): pl.pallas_call(kernel, out_shape=(out, out), in_specs=[pl.BlockSpec(memor...]
    all_gather x2 -> x0, blocking collectives: 36.5 us -> none  [entering(): pieces = jax.tree.map(lambda part: lax.all_gather(part, axis), value)]
    dot_general x1 -> x0, matrix products: 32.4 us -> none  [shards(): jnp.einsum('ph,vprc->rvhc', sky_shard_values, coefficients, preferred_ele...]
    select_n x15 -> x2, other arithmetic: 19.3 us -> 0.72 us  [fused(): sky = jnp.take(sky_year, hour_list, axis=1).T]
    add x15 -> x0, other arithmetic: 14.8 us -> none  [the longest x6 6.23 us: shards(): lax.associative_scan(combine, (retain_rates, luminance), reverse=True, ax...]
    pad x8 -> x0, local copies, waits for them, and re-layouts: 13.3 us -> none  [the longest x4 6.65 us: shards(): lax.associative_scan(combine, (retain_rates, luminance), reverse=True, ax...]
    ppermute x2 -> x0, starting transfers between devices: 5.55 us -> none  [the longest x1 2.84 us: padded_2(): lax.ppermute(lax.slice_in_dim(block, 0, width, axis=dim), axis, backward)]
  transfers between devices with their start and end apart: 5 -> 0, of which waited for: 1 -> 0; matrix products, arithmetic and copies ran while one was open for 12% -> 0% of each run, Pallas kernels for 0% -> 0%
where the time goes in v1:
time: 77.2 us; the launch traced here: 76.8 us
  Pallas kernels  57.2 us (74%)
  local copies, waits for them, and re-layouts  18.2 us (24%)
    pallas_call x1, Pallas kernels, fused(): pl.pallas_call(kernel, out_shape=(out, out), in_specs=[pl.BlockSpec(memor...  57.2 us
    unnamed x5, local copies, waits for them, and re-layouts  13.7 us
    gather x1, local copies, waits for them, and re-layouts, fused(): sky = jnp.take(sky_year, hour_list, axis=1).T  4.55 us

profile of v1, /device:TPU:5, one launch (start us, length us, event | category | flops | bytes accessed | tf_op | source)
XLA Modules:
  0.0 76.8 jit_solution(1599607227121786250)
XLA Ops:
  0.6 0.0 copy-start
  0.6 8.3 %copy.6 = bf16[288,8760]{0,1:T(8,128)(2,1)} copy(bf16[288,8760]{1,0:T(8,128)(2,1)} %param.5) | data formatting | bytes 10091520 | tf_op args[1]
  9.0 0.0 copy-done
  9.0 4.5 %gather_fusion = bf16[96,288]{1,0:T(8,128)(2,1)S(1)} fusion(bf16[288,8760]{0,1:T(8,128)(2,1)} %copy.6, s32[1024]{0:T(1024)S(1)} %pad_clamp_fusion), kind=kCustom, calls=%fused_computation | custom fusion | bytes 110976 | tf_op jit(solution)/shard_map/jit(_take)/gather | solution.py:521
  13.6 0.7 broadcast_select_fusion.sky_ref
  14.3 57.2 %shard_map.59 = (f32[4,2,96,512]{3,2,1,0:T(8,128)}, f32[4,2,96,512]{3,2,1,0:T(8,128)}) custom-call(bf16[96,288]{1,0:T(8,128)(2,1)} %broadcast_select_fusion.sky_ref, bf16[2,288,32,512]{3,2,1,0:T(8,128)(2,1)} %coef_ref.1, f32[4,512]{1,0:T(4,128)} %ret_ref.1), custom_call_target="tpu_custom_call" | custom-call | tf_op jit(solution)/shard_map/pallas_call | solution.py:531
  71.5 2.7 %copy.9 = f32[4,2,96,512]{3,2,1,0:T(8,128)} copy(f32[4,2,96,512]{3,2,1,0:T(8,128)} %get-tuple-element.4) | data formatting | bytes 3145728
  74.1 2.7 %copy.10 = f32[4,2,96,512]{3,2,1,0:T(8,128)} copy(f32[4,2,96,512]{3,2,1,0:T(8,128)} %get-tuple-element.5) | data formatting | bytes 3145728
  (3 shorter events, 0.0 us)
Async XLA Ops:
  0.6 8.4 %copy-start = (s32[96]{0:T(128)S(1)}, s32[96]{0:T(128)}, u32[]{:S(2)}) copy-start(s32[96]{0:T(128)} %param.6) | copy-start | bytes 1156

commit v2 on v1

--- a/solution.py
+++ b/solution.py
@@ -195,83 +195,85 @@
             device_id_type=MESH,
         )
 
-    def hop(k, n):
+    def hop(k, n, piece, first, count):
         target = chip_of(n, core) * 2 + core
         return [
             pltpu.make_async_remote_copy(
-                src_ref=src.at[k],
-                dst_ref=dst.at[k],
-                send_sem=hop_sem.at[0, i, k],
-                recv_sem=hop_sem.at[1, i, k],
+                src_ref=src.at[k, pl.ds(first, count)],
+                dst_ref=dst.at[k, pl.ds(first, count)],
+                send_sem=hop_sem.at[0, i, piece],
+                recv_sem=hop_sem.at[1, i, piece],
                 device_id=at(target),
                 device_id_type=MESH,
             )
             for i, (src, dst) in enumerate(((code_out, code_in), (top_out, top_in)))
         ]
 
-    @pl.loop(0, chips)
-    def _(k):
+    half = rows // 2
+    edges = rows - 2
+
+    def hop_half(k, h):
+        return hop(k, 1, 2 * k + h, h * half, half)
+
+    second = ((4, 0, 2), (5, edges, 2), (6, 2, rows - 4))
+
+    def unit(k, more):
         load(other, chip_of(k, other), 0).wait()
         product(0, given, k)
         pair(k).start()
-
-        @pl.when(k < chips - 1)
-        def _():
+        if more:
             load(other, chip_of(k + 1, other), 0).start()
-
         load(core, chip_of(k, core), 1).wait()
         product(1, mine, k)
-
-        @pl.when(k < chips - 1)
-        def _():
+        if more:
             load(core, chip_of(k + 1, core), 1).start()
+
+    @pl.loop(0, chips - 1)
+    def _(k):
+        unit(k, True)
 
         @pl.when(k < 2)
         def _():
             pair(k).wait_recv()
-
-            @pl.loop(0, rows)
-            def _(r):
-                code, top = encode(mine[k, r] + taken[k, r])
-                code_out[k, r] = code
-                top_out[k, pl.ds(r, 1), :] = top
-
-            for copy in hop(k, 1):
-                copy.start()
+            for h in range(2):
+                @pl.loop(h * half, h * half + half)
+                def _(r):
+                    code, top = encode(mine[k, r] + taken[k, r])
+                    code_out[k, r] = code
+                    top_out[k, r] = top
+
+                for copy in hop_half(k, h):
+                    copy.start()
 
     pair(2).wait_recv()
-    for copy in hop(0, 1):
-        copy.wait_recv()
-
-    @pl.loop(0, rows)
-    def _(r):
-        came = decode(code_in[0, r], top_in[0, pl.ds(r, 1), :])
-        code, top = encode(mine[2, r] + taken[2, r] + came)
-        code_out[2, r] = code
-        top_out[2, pl.ds(r, 1), :] = top
-
-    for copy in hop(2, 2):
-        copy.start()
-
+    for piece, first, count in second:
+        if piece < 6:
+            for copy in hop_half(0, piece - 4):
+                copy.wait_recv()
+
+        @pl.loop(first, first + count)
+        def _(r):
+            came = decode(code_in[0, r], top_in[0, r])
+            code, top = encode(mine[2, r] + taken[2, r] + came)
+            code_out[2, r] = code
+            top_out[2, r] = top
+
+        for copy in hop(2, 2, piece, first, count):
+            copy.start()
+
+    unit(chips - 1, False)
     pair(3).wait_recv()
-    for copy in hop(1, 1):
-        copy.wait_recv()
-
-    @pl.loop(0, rows)
-    def _(r):
-        came = decode(code_in[1, r], top_in[1, pl.ds(r, 1), :])
-        mine[3, r] = mine[3, r] + taken[3, r] + came
+    for h in range(2):
+        for copy in hop_half(1, h):
+            copy.wait_recv()
+
+        @pl.loop(h * half, h * half + half)
+        def _(r):
+            came = decode(code_in[1, r], top_in[1, r])
+            mine[3, r] = mine[3, r] + taken[3, r] + came
 
     for copy in ret_copies:
         copy.wait()
-
-    for copy in hop(2, 2):
-        copy.wait_recv()
-
-    @pl.loop(0, rows)
-    def _(r):
-        came = decode(code_in[2, r], top_in[2, pl.ds(r, 1), :])
-        lum[r + 2] = mine[3, r] + came
 
     def halo(way, i):
         target = (chip + (1 - 2 * way) + chips) % chips * 2 + core
@@ -296,18 +298,19 @@
     not_last = chip < chips - 1
     not_first = chip > 0
 
-    @pl.when(not_last)
-    def _():
-        send_halo(0)
-
-    @pl.when(not_first)
-    def _():
-        send_halo(1)
-
-    def rate(r):
-        return rets[chip * 2 + r // 4, pl.ds(r % 4, 1), :]
-
-    half = rows // 2
+    for piece, first, count in second:
+        for copy in hop(2, 2, piece, first, count):
+            copy.wait_recv()
+
+        @pl.loop(first, first + count)
+        def _(r):
+            came = decode(code_in[2, r], top_in[2, r])
+            lum[r + 2] = mine[3, r] + came
+
+        if piece < 6:
+            @pl.when(not_last if piece == 5 else not_first)
+            def _():
+                send_halo(5 - piece)
 
     def rate(r):
         return rets[chip * 2 + r // half, pl.ds(r % half, 1), :]
@@ -487,8 +490,13 @@
     def _(k):
         pair(k).wait_send()
 
-    for k, n in ((0, 1), (1, 1), (2, 2)):
-        for copy in hop(k, n):
+    for k in range(2):
+        for h in range(2):
+            for copy in hop_half(k, h):
+                copy.wait_send()
+
+    for piece, first, count in second:
+        for copy in hop(2, 2, piece, first, count):
             copy.wait_send()
 
     @pl.when(not_last)
@@ -518,7 +526,11 @@
 
 
 def fused(coefficients, sky_year, hour_list, retention):
-    sky = jnp.take(sky_year, hour_list, axis=1).T
+    year = lax.broadcasted_iota(jnp.int32, (hour_list.shape[0], sky_year.shape[1]), 1)
+    picks = (year == hour_list[:, None]).astype(jnp.bfloat16)
+    sky = jnp.einsum(
+        "hy,py->hp", picks, sky_year, preferred_element_type=jnp.float32
+    ).astype(jnp.bfloat16)
     views, depth, all_rows, columns = coefficients.shape
     hours = sky.shape[0]
     half = retention.shape[0]
@@ -544,9 +556,9 @@
             pltpu.VMEM((chips,) + image, f32),
             pltpu.VMEM((chips,) + image, f32),
             pltpu.VMEM((3,) + image, bf16),
-            pltpu.VMEM((3, rows, columns), f32),
+            pltpu.VMEM((3, rows, 1, columns), f32),
             pltpu.VMEM((3,) + image, bf16),
-            pltpu.VMEM((3, rows, columns), f32),
+            pltpu.VMEM((3, rows, 1, columns), f32),
             pltpu.VMEM((rows + 4, hours, columns), f32),
             pltpu.VMEM((2, 2, hours, columns), bf16),
             pltpu.VMEM((2, 2, 1, columns), f32),
@@ -563,14 +575,14 @@
             dma((2,)),
             dma((2, 2 * chips)),
             dma((2, chips)),
-            dma((2, 2, 3)),
+            dma((2, 2, 7)),
             dma((2, 2, 2)),
             dma((2, 2, chips)),
             dma((2, 2)),
             dma((2,)),
         ],
         compiler_params=pltpu.CompilerParams(
-            collective_id=0, has_side_effects=True, vmem_limit_bytes=60 * 1024 * 1024
+            collective_id=0, has_side_effects=True, vmem_limit_bytes=48 * 1024 * 1024
         ),
     )(sky, coefficients, retention)
 

time: 77.2 us -> 60.4 us (0.78)
  local copies, waits for them, and re-layouts: 18.2 us -> 2.29 us
  matrix products: 0 us -> 4.36 us
  Pallas kernels: 57.2 us -> 52.9 us
    unnamed x5 -> x4, local copies, waits for them, and re-layouts: 13.7 us -> 2.29 us
    gather x1 -> x0, local copies, waits for them, and re-layouts: 4.55 us -> none  [fused(): sky = jnp.take(sky_year, hour_list, axis=1).T]
    dot_general x0 -> x1, matrix products: none -> 4.36 us  [fused(): jnp.einsum('hy,py->hp', picks, sky_year, preferred_element_type=jnp.float32)]
    pallas_call x1, Pallas kernels: 57.2 us -> 52.9 us  [fused(): pl.pallas_call(kernel, out_shape=(out, out), in_specs=[pl.BlockSpec(memor...]
where the time goes in v2:
time: 60.4 us; the launch traced here: 60.2 us
  Pallas kernels  52.9 us (88%)
  matrix products  4.36 us (7%)
  local copies, waits for them, and re-layouts  2.29 us (4%)
  between operations  0.66 us (1%)
    pallas_call x1, Pallas kernels, fused(): pl.pallas_call(kernel, out_shape=(out, out), in_specs=[pl.BlockSpec(memor...  52.9 us
    dot_general x1, matrix products, fused(): jnp.einsum('hy,py->hp', picks, sky_year, preferred_element_type=jnp.float32)  4.36 us
    unnamed x4, local copies, waits for them, and re-layouts  2.29 us

profile of v2, /device:TPU:5, one launch (start us, length us, event | category | flops | bytes accessed | tf_op | source)
XLA Modules:
  0.0 60.2 jit_solution(9255973870765805383)
XLA Ops:
  0.6 0.0 copy-start
  0.6 4.4 %fusion.2.sky_ref = bf16[96,288]{1,0:T(8,128)(2,1)S(1)} fusion(bf16[288,8760]{1,0:T(8,128)(2,1)} %param.5, s32[96]{0:T(128)} %param.6), kind=kOutput, calls=%fused_computation.3 | convolution fusion | flops 485261568 | bytes 5101440 | tf_op jit(solution)/shard_map/hy,py->hp/dot_general | solution.py:531
  5.0 0.0 copy-done
  5.0 52.9 %shard_map.59 = (f32[4,2,96,512]{3,2,1,0:T(8,128)S(1)}, f32[4,2,96,512]{3,2,1,0:T(8,128)S(1)}) custom-call(bf16[96,288]{1,0:T(8,128)(2,1)S(1)} %fusion.2.sky_ref, bf16[2,288,32,512]{3,2,1,0:T(8,128)(2,1)} %coef_ref.1, f32[4,512]{1,0:T(4,128)S(1)} %copy-done), custom_call_target="tpu_custom_call" | custom-call | tf_op jit(solution)/shard_map/pallas_call | solution.py:543
  58.0 1.1 %copy.8 = f32[4,2,96,512]{3,2,1,0:T(8,128)} copy(f32[4,2,96,512]{3,2,1,0:T(8,128)S(1)} %get-tuple-element.4) | data formatting | bytes 3145728
  59.1 1.1 %copy.9 = f32[4,2,96,512]{3,2,1,0:T(8,128)} copy(f32[4,2,96,512]{3,2,1,0:T(8,128)S(1)} %get-tuple-element.5) | data formatting | bytes 3145728
Async XLA Ops:
  0.6 4.4 %copy-start = (f32[4,512]{1,0:T(4,128)S(1)}, f32[4,512]{1,0:T(4,128)}, u32[]{:S(2)}) copy-start(f32[4,512]{1,0:T(4,128)} %ret_ref.1) | copy-start | bytes 24580
